TPU v7x, 128 devices: a whole 4x4x4 slice. The times are simulated.
128 devices in a mesh: rel: 4 (over z), ent: 32 (over y, x, core).
Axes of the slice: x: 4, y: 4, z: 4, core: 2. Of those that a mesh axis runs over, the one named last changes fastest.
Arguments:
- features: bfloat16 [16384, 512], P('ent'), may hold values from -6 to 6
- w_self: bfloat16 [512, 512], replicated, may hold values from -0.25 to 0.25
- basis_mats: bfloat16 [16384, 512], replicated, may hold values from -0.046875 to 0.046875
- basis_coeffs: float32 [1000, 32], replicated, may hold values from -5 to 5
- group_rels: int32 [1000], P('rel'), may hold values from 0 to 999, each once
- rel_local: int32 [65536], P(('rel', 'ent')), may hold values from 0 to 249
- edge_src: int32 [65536], P(('rel', 'ent')), may hold values from 0 to 16383, as said below
- edge_dst: int32 [65536], P(('rel', 'ent')), may hold values from 0 to 16383, as said below
- block_counts: int32 [4, 32, 32], P('rel', 'ent'), may hold values from 1 to 16, as said below
- cotangent: bfloat16 [16384, 512], P('ent'), may hold values from -6 to 6
Outputs:
- activations: bfloat16 [16384, 512], P('ent')
- grad_features: bfloat16 [16384, 512], P('ent')
- grad_basis: float32 [16384, 512], P(('rel', 'ent'))
Inputs may be any that keep to these rules, and one draw needn't show every extreme that they name: `edge_src`: slot i's source is owned by ent index (i // 512) % 32: it lies in [that index * 512, that index * 512 + 512). `edge_dst`: slot i's destination is owned by block index k = (i % 512) // 16: it lies in [k * 512, k * 512 + 512); within each aligned block of 16 slots the destinations are non-decreasing; the live slots of a block are its first block_counts ones. `block_counts`: one relation group, drawn from the seed, has every block full.
All inputs are finite; a program needn't handle non-finite values.
Results may differ from a plain program's by a relative error of at most 0.0059.
Values may be sent and summed in bfloat16 or wider, within the bound.
A program may use at most 192 MiB of HBM per device.

v0:
```python
import jax
import jax.numpy as jnp
from jax import lax
from jax.sharding import PartitionSpec as P

BF = jnp.bfloat16
F32 = jnp.float32


def dot(a, b, dims=((1,), (0,)), precision=None):
    return lax.dot_general(a, b, (dims, ((), ())), preferred_element_type=F32, precision=precision)


def swap(x, axis):
    return lax.all_to_all(x, axis, split_axis=0, concat_axis=0, tiled=True)


def per_device(
    features,
    w_self,
    basis_mats,
    basis_coeffs,
    group_rels,
    rel_local,
    edge_src,
    edge_dst,
    block_counts,
    cotangent,
):
    n_ent, width = features.shape
    ent_count = lax.axis_size("ent")
    rel_count = lax.axis_size("rel")
    slots = rel_local.shape[0]
    cap = slots // ent_count
    bases = basis_coeffs.shape[1]
    rels = basis_coeffs.shape[0]
    part = width // rel_count
    q = lax.axis_index("rel")
    s = lax.axis_index("ent")
    all_slots = slots * rel_count
    pos = jnp.arange(slots, dtype=jnp.int32)
    limits = jnp.repeat(block_counts.reshape(ent_count), cap, total_repeat_length=slots)
    live = pos % cap < limits
    src_own = edge_src - s * n_ent
    dst_own = jnp.where(live, edge_dst - pos // cap * n_ent, n_ent)
    rel_own = group_rels[rel_local]
    meta = jnp.stack([src_own, dst_own, rel_own])
    meta = lax.all_gather(meta, "rel").reshape(rel_count, 3, ent_count, cap)
    meta = meta.transpose(2, 1, 0, 3)
    src = meta[:, 0].reshape(all_slots)
    arrived = swap(meta[:, 1:], "ent")
    dst = arrived[:, 0].reshape(all_slots)
    rel = arrived[:, 1].reshape(all_slots)
    ids = jnp.arange(n_ent, dtype=jnp.int32)[:, None]
    pick_src = (ids == src[None, :]).astype(BF)
    feat_part = lax.dynamic_slice_in_dim(features, q * part, part, 1)
    rows = dot(pick_src, feat_part, ((0,), (0,))).astype(BF)
    rows = swap(rows.reshape(ent_count, rel_count * cap, part), "ent").reshape(all_slots, part)
    pick_rel = (jnp.arange(rels, dtype=jnp.int32)[:, None] == rel[None, :]).astype(F32)
    coef_t = dot(basis_coeffs, pick_rel, ((0,), (0,)), lax.Precision.HIGHEST)
    pick = (ids == dst[None, :]).astype(BF)
    degree = jnp.sum(pick, axis=1, dtype=F32)
    inverse = (1.0 / jnp.maximum(degree, 1.0))[:, None]
    mixed_t = (
        (coef_t[:, None, :] * rows.T.astype(F32)[None]).reshape(bases * part, all_slots).astype(BF)
    )
    agg = dot(pick, mixed_t, ((1,), (1,))).astype(BF)
    basis_part = lax.dynamic_slice_in_dim(
        basis_mats.reshape(bases, width, width), q * part, part, 1
    ).reshape(bases * part, width)
    partial = dot(agg, basis_part).astype(BF)
    partial = swap(partial.reshape(n_ent, rel_count, part).transpose(1, 0, 2), "rel")
    sums = jnp.sum(partial.astype(F32), axis=0)
    w_part = lax.dynamic_slice_in_dim(w_self, q * part, part, 1)
    cot = lax.dynamic_slice_in_dim(cotangent, q * part, part, 1).astype(F32)
    pre = dot(features, w_part) + sums * inverse
    sig = jax.nn.sigmoid(pre)
    act = (pre * sig).astype(BF)
    grad_pre = (cot * (sig * (1.0 + pre * (1.0 - sig)))).astype(BF)
    act = lax.all_gather(act, "rel", axis=1, tiled=True)
    grad_pre = lax.all_gather(grad_pre, "rel", axis=1, tiled=True)
    scaled = (grad_pre.astype(F32) * inverse).astype(BF)
    basis_terms = dot(agg, scaled, ((0,), (0,))).astype(BF)
    basis_terms = swap(basis_terms.reshape(ent_count, part, width), "ent")
    block = jnp.sum(basis_terms.astype(F32), axis=0)
    per_rel = bases // rel_count
    routes = [
        (r * ent_count + b, b // per_rel * ent_count + b % per_rel * rel_count + r)
        for r in range(rel_count)
        for b in range(bases)
    ]
    grad_basis = lax.ppermute(block, ("rel", "ent"), routes)
    back_t = dot(basis_part, scaled, ((1,), (1,))).astype(BF)
    spread = dot(back_t, pick).reshape(bases, part, all_slots)
    grad_rows = jnp.sum(spread * coef_t[:, None, :], axis=0).astype(BF).T
    grad_rows = swap(grad_rows.reshape(ent_count, rel_count * cap, part), "ent")
    w_rows = lax.dynamic_slice_in_dim(w_self, q * part, part, 0)
    grad_part = dot(grad_pre, w_rows, ((1,), (1,))) + dot(
        pick_src, grad_rows.reshape(all_slots, part)
    )
    grad_features = lax.all_gather(grad_part.astype(BF), "rel", axis=1, tiled=True)
    return (act, grad_features, grad_basis)


def solution(mesh):
    placed = (
        P("ent", None),
        P(),
        P(),
        P(),
        P("rel"),
        P(("rel", "ent")),
        P(("rel", "ent")),
        P(("rel", "ent")),
        P("rel", "ent", None),
        P("ent", None),
    )
    return jax.shard_map(
        per_device,
        mesh=mesh,
        in_specs=placed,
        out_specs=(P("ent", None), P("ent", None), P(("rel", "ent"), None)),
        check_vma=False,
    )
```

profile of v0, /device:TPU:27, one launch (start us, length us, event | category | flops | bytes accessed | tf_op | source)
XLA Modules:
  0.0 229.3 jit_solution(15646126451064702323)
XLA Ops:
  6.0 4.5 %compare_select_fusion.1 = (s32[512,1]{0,1:T(1,128)S(1)}, s32[512,1]{0,1:T(1,128)S(1)}) fusion(s32[]{:T(128)} %bitcast.31, s32[]{:T(128)} %bitcast.32, s32[]{:T(128)} %bitcast.33, s32[]{:T(128)} %bitcast.34, s32[]{:T(128)} %bitcast.35, s32[]{:T(128)} %bitcast.37, s32[]{:T(128)} %bitcast.36, s32[512,1]{0,1:T(1,128)S(1)} %bitcast.106, s32[512,1]{0,1:T(1,128)S(1)} %bitcast.105), kind=kLoop, calls=%fused_computation.66 | loop fusion | flops 7168 | bytes 8220 | tf_op jit(solution)/shard_map/jit(_take)/gather | solution.py:42
  11.4 3.6 %gather_fusion = s32[512]{0:T(512)S(1)} fusion(s32[250]{0:T(256)} %param.16, s32[1024]{0:T(1024)S(1)} %pad_clamp_fusion), kind=kCustom, calls=%fused_computation | custom fusion | bytes 6144 | tf_op jit(solution)/shard_map/gather | solution.py:46
  15.0 16.4 %fusion.23 = s32[512]{0:T(512)S(1)} fusion(s32[512]{0:T(512)} %param.19, pred[512]{0:T(512)(128)(4,1)S(1)} %get-tuple-element.51, pred[512]{0:T(512)(128)(4,1)S(1)} %get-tuple-element.50, pred[512]{0:T(512)(128)(4,1)S(1)} %get-tuple-element.49, pred[512]{0:T(512)(128)(4,1)S(1)} %get-tuple-element.48, pred[512]{0:T(512)(128)(4,1)S(1)} %get-tuple-element.47, ...), kind=kLoop, calls=%fused_computation.85 | loop fusion | flops 25600 | bytes 21108 | tf_op jit(solution)/shard_map/jit(_where)/select_n | solution.py:45
  31.4 10.5 %all-gather.1 = s32[4,3,512]{2,1,0:T(4,128)S(1)} all-gather(s32[1,3,512]{2,1,0:T(4,128)S(1)} %add_bitcast_fusion), channel_id=2, replica_groups=mesh['rel'=4,'ent'=32] {'rel'}, dimensions={0}, use_global_device_ids=true | all-gather | bytes 30720 | tf_op jit(solution)/shard_map/all_gather | solution.py:48
  42.9 10.3 %all-to-all-start = ((s32[32,1,128]{2,1,0:T(1,128)}), s32[32,1,128]{2,1,0:T(1,128)S(1)}, u32[]{:S(2)}, u32[]{:S(2)}) async-start(s32[32,1,128]{2,1,0:T(1,128)} %reshape.365), calls=%async_computation | async-start | bytes 32768 | tf_op jit(solution)/shard_map/all_to_all | solution.py:15
  57.3 7.0 %all-to-all-start.1 = ((bf16[32,64,128]{2,1,0:T(8,128)(2,1)}), bf16[32,64,128]{2,1,0:T(8,128)(2,1)S(1)}, u32[]{:S(2)}, u32[]{:S(2)}) async-start(bf16[32,64,128]{2,1,0:T(8,128)(2,1)} %bitcast.44), calls=%async_computation.1 | async-start | bytes 1048576 | tf_op jit(solution)/shard_map/all_to_all | solution.py:15
  64.3 4.6 %constant_dynamic-slice_fusion.1 = bf16[32,128,512]{2,1,0:T(8,128)(2,1)} fusion(bf16[32,512,512]{2,1,0:T(8,128)(2,1)} %bitcast.98, s32[]{:T(128)S(6)} %select_n.47), kind=kLoop, calls=%fused_computation.95 | loop fusion | bytes 8388612 | tf_op jit(solution)/shard_map/dynamic_slice | solution.py:68
  70.5 3.0 %fusion.7 = f32[32,2048]{1,0:T(8,128)S(1)} fusion(f32[1000,32]{0,1:T(8,128)S(1)} %copy-done.4, s32[2048]{0:T(1024)S(1)} %eq.52), kind=kOutput, calls=%fused_computation.18 | convolution fusion | flops 788480000 | bytes 398336 | tf_op jit(solution)/shard_map/dot_general | solution.py:11
  73.9 6.8 %multiply_convert_fusion = bf16[32,128,2048]{2,1,0:T(8,128)(2,1)} fusion(f32[128,2048]{1,0:T(8,128)S(1)} %bitcast.93, f32[32,2048]{1,0:T(8,128)S(1)} %fusion.7), kind=kLoop, calls=%fused_computation.2 | loop fusion | flops 16777216 | bytes 18087936 | tf_op jit(solution)/shard_map/convert_element_type | solution.py:65
  80.8 13.9 %convolution_convert_fusion = bf16[512,4096]{1,0:T(8,128)(2,1)} fusion(bf16[4096,2048]{1,0:T(8,128)(2,1)} %bitcast.92, s32[2048]{0:T(1024)S(1)} %eq.48), kind=kOutput, calls=%fused_computation.6 | convolution fusion | flops 8593080320 | bytes 20979712 | tf_op jit(solution)/shard_map/dot_general | solution.py:11
  94.7 5.5 %convolution_convert_fusion.3 = bf16[512,512]{0,1:T(8,128)(2,1)} fusion(bf16[512,4096]{1,0:T(8,128)(2,1)} %convolution_convert_fusion, bf16[4096,512]{1,0:T(8,128)(2,1)S(1)} %bitcast.95), kind=kOutput, calls=%fused_computation.23 | convolution fusion | flops 2147745792 | bytes 8912896 | tf_op jit(solution)/shard_map/dot_general | solution.py:11
  100.1 3.8 %all-to-all-start.2 = ((bf16[4,512,128]{1,2,0:T(8,128)(2,1)}), bf16[4,512,128]{1,2,0:T(8,128)(2,1)S(1)}, u32[]{:S(2)}, u32[]{:S(2)}) async-start(bf16[4,512,128]{1,2,0:T(8,128)(2,1)} %bitcast.51), calls=%async_computation.2 | async-start | bytes 1048576 | tf_op jit(solution)/shard_map/all_to_all | solution.py:15
  105.5 7.4 %all-to-all-done.2 = bf16[4,512,128]{1,2,0:T(8,128)(2,1)S(1)} async-done(((bf16[4,512,128]{1,2,0:T(8,128)(2,1)}), bf16[4,512,128]{1,2,0:T(8,128)(2,1)S(1)}, u32[]{:S(2)}, u32[]{:S(2)}) %all-to-all-start.2) | async-done | bytes 524320 | tf_op jit(solution)/shard_map/all_to_all | solution.py:15
  113.4 10.7 %all_gather.18 = bf16[512,512]{0,1:T(8,128)(2,1)S(1)} all-gather(bf16[512,128]{0,1:T(8,128)(2,1)S(1)} %get-tuple-element.54), channel_id=1, replica_groups=mesh['rel'=4,'ent'=32] {'rel'}, dimensions={1}, use_global_device_ids=true | all-gather | bytes 655360 | tf_op jit(solution)/shard_map/all_gather | solution.py:81
  124.1 6.6 %convolution_convert_fusion.1 = bf16[4096,512]{1,0:T(8,128)(2,1)} fusion(bf16[512,4096]{1,0:T(8,128)(2,1)} %convolution_convert_fusion, bf16[512,512]{0,1:T(8,128)(2,1)S(1)} %all_gather.18, f32[512]{0:T(512)S(1)} %maximum_divide_fusion), kind=kOutput, calls=%fused_computation.7 | convolution fusion | flops 2150367232 | bytes 8914944 | tf_op jit(solution)/shard_map/dot_general | solution.py:11
  130.8 11.3 %all-to-all-start.4 = ((bf16[32,128,512]{2,1,0:T(8,128)(2,1)}), bf16[32,128,512]{2,1,0:T(8,128)(2,1)}, u32[]{:S(2)}, u32[]{:S(2)}) async-start(bf16[32,128,512]{2,1,0:T(8,128)(2,1)} %bitcast.96), calls=%async_computation.4 | async-start | bytes 8388608 | tf_op jit(solution)/shard_map/all_to_all | solution.py:15
  142.1 11.1 %all_gather.17 = bf16[512,512]{0,1:T(8,128)(2,1)S(1)} all-gather(bf16[512,128]{0,1:T(8,128)(2,1)S(1)} %get-tuple-element.55), channel_id=1, replica_groups=mesh['rel'=4,'ent'=32] {'rel'}, dimensions={1}, use_global_device_ids=true | all-gather | bytes 655360 | tf_op jit(solution)/shard_map/all_gather | solution.py:80
  154.2 4.5 %convolution_convert_fusion.2.clone.5 = bf16[4096,512]{1,0:T(8,128)(2,1)S(1)} fusion(bf16[4096,512]{1,0:T(8,128)(2,1)} %bitcast.94, bf16[512,512]{0,1:T(8,128)(2,1)S(1)} %all_gather.18, f32[512]{0:T(512)S(1)} %maximum_divide_fusion), kind=kOutput, calls=%fused_computation.8.clone.clone.clone.2 | convolution fusion | flops 2150367232 | bytes 8914944 | tf_op jit(solution)/shard_map/dot_general | solution.py:11
  158.7 14.6 %fusion.3 = f32[4096,2048]{1,0:T(8,128)} fusion(s32[2048]{0:T(1024)S(1)} %eq.48, bf16[4096,512]{1,0:T(8,128)(2,1)S(1)} %convolution_convert_fusion.2.clone.5), kind=kOutput, calls=%fused_computation.14 | convolution fusion | flops 8590983168 | bytes 37756928 | tf_op jit(solution)/shard_map/dot_general | solution.py:11
  173.3 12.5 %multiply_reduce_fusion = bf16[128,2048]{1,0:T(8,128)(2,1)S(1)} fusion(f32[32,128,2048]{2,1,0:T(8,128)} %bitcast.91, f32[32,2048]{1,0:T(8,128)S(1)} %fusion.7), kind=kLoop, calls=%fused_computation.1 | loop fusion | flops 16515072 | bytes 34340864 | tf_op jit(solution)/shard_map/reduce_sum | solution.py:95
  186.8 5.1 %all-to-all-done.4 = bf16[32,128,512]{2,1,0:T(8,128)(2,1)} async-done(((bf16[32,128,512]{2,1,0:T(8,128)(2,1)}), bf16[32,128,512]{2,1,0:T(8,128)(2,1)}, u32[]{:S(2)}, u32[]{:S(2)}) %all-to-all-start.4) | async-done | bytes 4194336 | tf_op jit(solution)/shard_map/all_to_all | solution.py:15
  191.9 7.6 %all-to-all-start.3 = ((bf16[32,64,128]{2,1,0:T(8,128)(2,1)}), bf16[32,64,128]{2,1,0:T(8,128)(2,1)S(1)}, u32[]{:S(2)}, u32[]{:S(2)}) async-start(bf16[32,64,128]{2,1,0:T(8,128)(2,1)} %bitcast.54), calls=%async_computation.3 | async-start | bytes 1048576 | tf_op jit(solution)/shard_map/all_to_all | solution.py:15
  202.7 4.7 %collective-permute-start = (f32[128,512]{1,0:T(8,128)S(1)}, f32[128,512]{1,0:T(8,128)S(1)}, u32[]{:S(2)}, u32[]{:S(2)}) collective-permute-start(f32[128,512]{1,0:T(8,128)S(1)} %convert_reduce_fusion), channel_id=1, source_target_pairs={{0,0},{1,4},{2,8},{3,12},{4,16},{5,20},{6,24},{7,28},{8,32},{9,36}... | collective-permute-start | bytes 786440 | tf_op jit(solution)/shard_map/ppermute | solution.py:92
  209.5 18.3 %all_gather.19 = bf16[512,512]{1,0:T(8,128)(2,1)S(1)} all-gather(bf16[512,128]{1,0:T(8,128)(2,1)S(1)} %fusion.14), channel_id=1, replica_groups=mesh['rel'=4,'ent'=32] {'rel'}, dimensions={1}, use_global_device_ids=true | all-gather | bytes 655360 | tf_op jit(solution)/shard_map/all_gather | solution.py:101
  (53 shorter events, 24.1 us)
Async XLA Ops:
  0.6 52.7 %copy-start = (bf16[512,512]{1,0:T(8,128)(2,1)S(1)}, bf16[512,512]{1,0:T(8,128)(2,1)}, u32[]{:S(2)}) copy-start(bf16[512,512]{1,0:T(8,128)(2,1)} %param.12) | copy-start | bytes 1572868
  42.9 14.5 %all-to-all-start = ((s32[32,1,128]{2,1,0:T(1,128)}), s32[32,1,128]{2,1,0:T(1,128)S(1)}, u32[]{:S(2)}, u32[]{:S(2)}) async-start(s32[32,1,128]{2,1,0:T(1,128)} %reshape.365), calls=%async_computation | async-start | bytes 32768 | tf_op jit(solution)/shard_map/all_to_all | solution.py:15
  57.3 16.1 %all-to-all-start.1 = ((bf16[32,64,128]{2,1,0:T(8,128)(2,1)}), bf16[32,64,128]{2,1,0:T(8,128)(2,1)S(1)}, u32[]{:S(2)}, u32[]{:S(2)}) async-start(bf16[32,64,128]{2,1,0:T(8,128)(2,1)} %bitcast.44), calls=%async_computation.1 | async-start | bytes 1048576 | tf_op jit(solution)/shard_map/all_to_all | solution.py:15
  64.3 6.2 %copy-start.4 = (f32[1000,32]{0,1:T(8,128)S(1)}, f32[1000,32]{0,1:T(8,128)}, u32[]{:S(2)}) copy-start(f32[1000,32]{0,1:T(8,128)} %param.15) | copy-start | bytes 384004
  80.7 13.9 %copy-start.2 = (bf16[32,128,512]{2,1,0:T(8,128)(2,1)S(1)}, bf16[32,128,512]{2,1,0:T(8,128)(2,1)}, u32[]{:S(2)}) copy-start(bf16[32,128,512]{2,1,0:T(8,128)(2,1)} %constant_dynamic-slice_fusion.1) | copy-start | bytes 12582916
  94.7 18.3 %copy-start.3 = (bf16[512,512]{1,0:T(8,128)(2,1)S(1)}, bf16[512,512]{1,0:T(8,128)(2,1)}, u32[]{:S(2)}) copy-start(bf16[512,512]{1,0:T(8,128)(2,1)} %param.13) | copy-start | bytes 1572868
  100.1 12.8 %all-to-all-start.2 = ((bf16[4,512,128]{1,2,0:T(8,128)(2,1)}), bf16[4,512,128]{1,2,0:T(8,128)(2,1)S(1)}, u32[]{:S(2)}, u32[]{:S(2)}) async-start(bf16[4,512,128]{1,2,0:T(8,128)(2,1)} %bitcast.51), calls=%async_computation.2 | async-start | bytes 1048576 | tf_op jit(solution)/shard_map/all_to_all | solution.py:15
  130.8 61.1 %all-to-all-start.4 = ((bf16[32,128,512]{2,1,0:T(8,128)(2,1)}), bf16[32,128,512]{2,1,0:T(8,128)(2,1)}, u32[]{:S(2)}, u32[]{:S(2)}) async-start(bf16[32,128,512]{2,1,0:T(8,128)(2,1)} %bitcast.96), calls=%async_computation.4 | async-start | bytes 8388608 | tf_op jit(solution)/shard_map/all_to_all | solution.py:15
  191.9 16.7 %all-to-all-start.3 = ((bf16[32,64,128]{2,1,0:T(8,128)(2,1)}), bf16[32,64,128]{2,1,0:T(8,128)(2,1)S(1)}, u32[]{:S(2)}, u32[]{:S(2)}) async-start(bf16[32,64,128]{2,1,0:T(8,128)(2,1)} %bitcast.54), calls=%async_computation.3 | async-start | bytes 1048576 | tf_op jit(solution)/shard_map/all_to_all | solution.py:15
  199.5 29.8 %copy-start.1 = (bf16[512,512]{1,0:T(8,128)(2,1)S(1)}, bf16[512,512]{1,0:T(8,128)(2,1)}, u32[]{:S(2)}) copy-start(bf16[512,512]{1,0:T(8,128)(2,1)} %param.12) | copy-start | bytes 1572868
  202.7 25.1 %collective-permute-start = (f32[128,512]{1,0:T(8,128)S(1)}, f32[128,512]{1,0:T(8,128)S(1)}, u32[]{:S(2)}, u32[]{:S(2)}) collective-permute-start(f32[128,512]{1,0:T(8,128)S(1)} %convert_reduce_fusion), channel_id=1, source_target_pairs={{0,0},{1,4},{2,8},{3,12},{4,16},{5,20},{6,24},{7,28},{8,32},{9,36}... | collective-permute-start | bytes 786440 | tf_op jit(solution)/shard_map/ppermute | solution.py:92
where the time goes:
time: 230 us; the launch traced here: 229 us
  matrix products  51.8 us (23%)
  blocking collectives  50.6 us (22%)
  other arithmetic  46.6 us (20%)
  starting transfers between devices  44.7 us (19%)
  local copies, waits for them, and re-layouts  19 us (8%)
  waiting for transfers between devices  15.7 us (7%)
    dot_general x10, matrix products, dot(): lax.dot_general(a, b, (dims, ((), ())), preferred_element_type=F32, preci...  51.8 us
    all_to_all x5, starting transfers between devices, swap(): return lax.all_to_all(x, axis, split_axis=0, concat_axis=0, tiled=True)  40 us
    all_gather x1, blocking collectives, per_device(): lax.all_gather(grad_part.astype(BF), 'rel', axis=1, tiled=True)  18.3 us
    select_n x1, other arithmetic, per_device(): dst_own = jnp.where(live, edge_dst - pos // cap * n_ent, n_ent)  16.4 us
    all_to_all x5, waiting for transfers between devices, swap(): return lax.all_to_all(x, axis, split_axis=0, concat_axis=0, tiled=True)  15.7 us
    reduce_sum x1, other arithmetic, per_device(): grad_rows = jnp.sum(spread * coef_t[:, None, :], axis=0).astype(BF).T  12.5 us
    all_gather x1, blocking collectives, per_device(): act = lax.all_gather(act, 'rel', axis=1, tiled=True)  11.1 us
    all_gather x1, blocking collectives, per_device(): grad_pre = lax.all_gather(grad_pre, 'rel', axis=1, tiled=True)  10.7 us
  transfers between devices with their start and end apart: 6, of which 4 were waited for; matrix products, arithmetic and copies ran while one was open for 22% of the time, Pallas kernels for 0%

commit v1 on v0

--- a/solution.py
+++ b/solution.py
@@ -27,6 +27,12 @@
     block_counts,
     cotangent,
 ):
+
+    def see_forms(own_rows):
+        n_chips = lax.psum(1, axis_name="rel")
+        side_arr = jnp.tile(own_rows, [n_chips if idx == 1 else 1 for idx in range(own_rows.ndim)])
+        return lax.all_to_all(side_arr, "rel", split_axis=1, concat_axis=1, tiled=True)
+
     n_ent, width = features.shape
     ent_count = lax.axis_size("ent")
     rel_count = lax.axis_size("rel")
@@ -98,7 +104,7 @@
     grad_part = dot(grad_pre, w_rows, ((1,), (1,))) + dot(
         pick_src, grad_rows.reshape(all_slots, part)
     )
-    grad_features = lax.all_gather(grad_part.astype(BF), "rel", axis=1, tiled=True)
+    grad_features = see_forms(grad_part.astype(BF))
     return (act, grad_features, grad_basis)
 
 

time: 230 us -> 270 us (1.17)
  the two profiles are of different devices: /device:TPU:27 before, /device:TPU:26 now
where the time goes in v1:
time: 270 us; the launch traced here: 269 us
  waiting for transfers between devices  61.5 us (23%)
  matrix products  51.7 us (19%)
  other arithmetic  46.7 us (17%)
  blocking collectives  44.5 us (16%)
  starting transfers between devices  43.3 us (16%)
  local copies, waits for them, and re-layouts  20.3 us (8%)
    all_to_all x5, waiting for transfers between devices, swap(): return lax.all_to_all(x, axis, split_axis=0, concat_axis=0, tiled=True)  61.5 us
    dot_general x10, matrix products, dot(): lax.dot_general(a, b, (dims, ((), ())), preferred_element_type=F32, preci...  51.7 us
    all_to_all x5, starting transfers between devices, swap(): return lax.all_to_all(x, axis, split_axis=0, concat_axis=0, tiled=True)  33.5 us
    all_gather x1, blocking collectives, per_device(): act = lax.all_gather(act, 'rel', axis=1, tiled=True)  17.9 us
    select_n x1, other arithmetic, per_device(): dst_own = jnp.where(live, edge_dst - pos // cap * n_ent, n_ent)  16.4 us
    all_gather x1, blocking collectives, per_device(): grad_pre = lax.all_gather(grad_pre, 'rel', axis=1, tiled=True)  13.4 us
    all_gather x1, blocking collectives, per_device(): meta = lax.all_gather(meta, 'rel').reshape(rel_count, 3, ent_count, cap)  13.1 us
    reduce_sum x1, other arithmetic, per_device(): grad_rows = jnp.sum(spread * coef_t[:, None, :], axis=0).astype(BF).T  12.5 us
  transfers between devices with their start and end apart: 7, of which 4 were waited for; matrix products, arithmetic and copies ran while one was open for 10% of the time, Pallas kernels for 0%

profile of v1, /device:TPU:26, one launch (start us, length us, event | category | flops | bytes accessed | tf_op | source)
XLA Modules:
  0.0 268.9 jit_solution(2613591434929838107)
XLA Ops:
  6.0 4.5 %compare_select_fusion.1 = (s32[512,1]{0,1:T(1,128)S(1)}, s32[512,1]{0,1:T(1,128)S(1)}) fusion(s32[]{:T(128)} %bitcast.31, s32[]{:T(128)} %bitcast.32, s32[]{:T(128)} %bitcast.33, s32[]{:T(128)} %bitcast.34, s32[]{:T(128)} %bitcast.35, s32[]{:T(128)} %bitcast.37, s32[]{:T(128)} %bitcast.36, s32[512,1]{0,1:T(1,128)S(1)} %bitcast.108, s32[512,1]{0,1:T(1,128)S(1)} %bitcast.107), kind=kLoop, calls=%fused_computation.66 | loop fusion | flops 7168 | bytes 8220 | tf_op jit(solution)/shard_map/jit(_take)/gather | solution.py:48
  11.4 3.6 %gather_fusion = s32[512]{0:T(512)S(1)} fusion(s32[250]{0:T(256)} %param.16, s32[1024]{0:T(1024)S(1)} %pad_clamp_fusion), kind=kCustom, calls=%fused_computation | custom fusion | bytes 6144 | tf_op jit(solution)/shard_map/gather | solution.py:52
  15.0 16.4 %fusion.23 = s32[512]{0:T(512)S(1)} fusion(s32[512]{0:T(512)} %param.19, pred[512]{0:T(512)(128)(4,1)S(1)} %get-tuple-element.54, pred[512]{0:T(512)(128)(4,1)S(1)} %get-tuple-element.53, pred[512]{0:T(512)(128)(4,1)S(1)} %get-tuple-element.52, pred[512]{0:T(512)(128)(4,1)S(1)} %get-tuple-element.51, pred[512]{0:T(512)(128)(4,1)S(1)} %get-tuple-element.50, ...), kind=kLoop, calls=%fused_computation.85 | loop fusion | flops 25600 | bytes 21108 | tf_op jit(solution)/shard_map/jit(_where)/select_n | solution.py:51
  31.4 13.1 %all-gather.1 = s32[4,3,512]{2,1,0:T(4,128)S(1)} all-gather(s32[1,3,512]{2,1,0:T(4,128)S(1)} %add_bitcast_fusion), channel_id=2, replica_groups=mesh['rel'=4,'ent'=32] {'rel'}, dimensions={0}, use_global_device_ids=true | all-gather | bytes 30720 | tf_op jit(solution)/shard_map/all_gather | solution.py:54
  45.5 7.3 %all-to-all-start = ((s32[32,1,128]{2,1,0:T(1,128)}), s32[32,1,128]{2,1,0:T(1,128)S(1)}, u32[]{:S(2)}, u32[]{:S(2)}) async-start(s32[32,1,128]{2,1,0:T(1,128)} %reshape.372), calls=%async_computation | async-start | bytes 32768 | tf_op jit(solution)/shard_map/all_to_all | solution.py:15
  57.3 6.7 %all-to-all-start.1 = ((bf16[32,64,128]{2,1,0:T(8,128)(2,1)}), bf16[32,64,128]{2,1,0:T(8,128)(2,1)S(1)}, u32[]{:S(2)}, u32[]{:S(2)}) async-start(bf16[32,64,128]{2,1,0:T(8,128)(2,1)} %bitcast.44), calls=%async_computation.1 | async-start | bytes 1048576 | tf_op jit(solution)/shard_map/all_to_all | solution.py:15
  64.0 4.6 %constant_dynamic-slice_fusion.1 = bf16[32,128,512]{2,1,0:T(8,128)(2,1)} fusion(bf16[32,512,512]{2,1,0:T(8,128)(2,1)} %bitcast.100, s32[]{:T(128)S(6)} %select_n.47), kind=kLoop, calls=%fused_computation.95 | loop fusion | bytes 8388612 | tf_op jit(solution)/shard_map/dynamic_slice | solution.py:74
  70.2 3.0 %fusion.7 = f32[32,2048]{1,0:T(8,128)S(1)} fusion(f32[1000,32]{0,1:T(8,128)S(1)} %copy-done.4, s32[2048]{0:T(1024)S(1)} %eq.52), kind=kOutput, calls=%fused_computation.18 | convolution fusion | flops 788480000 | bytes 398336 | tf_op jit(solution)/shard_map/dot_general | solution.py:11
  73.6 6.8 %multiply_convert_fusion = bf16[32,128,2048]{2,1,0:T(8,128)(2,1)} fusion(f32[128,2048]{1,0:T(8,128)S(1)} %bitcast.94, f32[32,2048]{1,0:T(8,128)S(1)} %fusion.7), kind=kLoop, calls=%fused_computation.2 | loop fusion | flops 16777216 | bytes 18087936 | tf_op jit(solution)/shard_map/convert_element_type | solution.py:71
  80.4 14.0 %convolution_convert_fusion = bf16[512,4096]{1,0:T(8,128)(2,1)} fusion(bf16[4096,2048]{1,0:T(8,128)(2,1)} %bitcast.93, s32[2048]{0:T(1024)S(1)} %eq.48), kind=kOutput, calls=%fused_computation.6 | convolution fusion | flops 8593080320 | bytes 20979712 | tf_op jit(solution)/shard_map/dot_general | solution.py:11
  94.4 5.5 %convolution_convert_fusion.3 = bf16[512,512]{0,1:T(8,128)(2,1)} fusion(bf16[512,4096]{1,0:T(8,128)(2,1)} %convolution_convert_fusion, bf16[4096,512]{1,0:T(8,128)(2,1)S(1)} %bitcast.96), kind=kOutput, calls=%fused_computation.23 | convolution fusion | flops 2147745792 | bytes 8912896 | tf_op jit(solution)/shard_map/dot_general | solution.py:11
  99.9 4.1 %all-to-all-start.2 = ((bf16[4,512,128]{1,2,0:T(8,128)(2,1)}), bf16[4,512,128]{1,2,0:T(8,128)(2,1)S(1)}, u32[]{:S(2)}, u32[]{:S(2)}) async-start(bf16[4,512,128]{1,2,0:T(8,128)(2,1)} %bitcast.51), calls=%async_computation.2 | async-start | bytes 1048576 | tf_op jit(solution)/shard_map/all_to_all | solution.py:15
  105.6 8.2 %all-to-all-done.2 = bf16[4,512,128]{1,2,0:T(8,128)(2,1)S(1)} async-done(((bf16[4,512,128]{1,2,0:T(8,128)(2,1)}), bf16[4,512,128]{1,2,0:T(8,128)(2,1)S(1)}, u32[]{:S(2)}, u32[]{:S(2)}) %all-to-all-start.2) | async-done | bytes 524320 | tf_op jit(solution)/shard_map/all_to_all | solution.py:15
  114.3 13.4 %all_gather.15 = bf16[512,512]{0,1:T(8,128)(2,1)S(1)} all-gather(bf16[512,128]{0,1:T(8,128)(2,1)S(1)} %get-tuple-element.57), channel_id=1, replica_groups=mesh['rel'=4,'ent'=32] {'rel'}, dimensions={1}, use_global_device_ids=true | all-gather | bytes 655360 | tf_op jit(solution)/shard_map/all_gather | solution.py:87
  127.8 4.5 %convolution_convert_fusion.2.clone.5 = bf16[4096,512]{1,0:T(8,128)(2,1)S(1)} fusion(bf16[4096,512]{1,0:T(8,128)(2,1)} %bitcast.95, bf16[512,512]{0,1:T(8,128)(2,1)S(1)} %all_gather.15, f32[512]{0:T(512)S(1)} %maximum_divide_fusion), kind=kOutput, calls=%fused_computation.8.clone.clone.clone.2 | convolution fusion | flops 2150367232 | bytes 8914944 | tf_op jit(solution)/shard_map/dot_general | solution.py:11
  132.3 14.6 %fusion.3 = f32[4096,2048]{1,0:T(8,128)} fusion(s32[2048]{0:T(1024)S(1)} %eq.48, bf16[4096,512]{1,0:T(8,128)(2,1)S(1)} %convolution_convert_fusion.2.clone.5), kind=kOutput, calls=%fused_computation.14 | convolution fusion | flops 8590983168 | bytes 37756928 | tf_op jit(solution)/shard_map/dot_general | solution.py:11
  146.9 12.5 %multiply_reduce_fusion = bf16[128,2048]{1,0:T(8,128)(2,1)S(1)} fusion(f32[32,128,2048]{2,1,0:T(8,128)} %bitcast.92, f32[32,2048]{1,0:T(8,128)S(1)} %fusion.7), kind=kLoop, calls=%fused_computation.1 | loop fusion | flops 16515072 | bytes 34340864 | tf_op jit(solution)/shard_map/reduce_sum | solution.py:101
  160.4 7.4 %all-to-all-start.3 = ((bf16[32,64,128]{2,1,0:T(8,128)(2,1)}), bf16[32,64,128]{2,1,0:T(8,128)(2,1)S(1)}, u32[]{:S(2)}, u32[]{:S(2)}) async-start(bf16[32,64,128]{2,1,0:T(8,128)(2,1)} %bitcast.54), calls=%async_computation.3 | async-start | bytes 1048576 | tf_op jit(solution)/shard_map/all_to_all | solution.py:15
  167.8 6.5 %convolution_convert_fusion.1 = bf16[4096,512]{1,0:T(8,128)(2,1)} fusion(bf16[512,4096]{1,0:T(8,128)(2,1)} %convolution_convert_fusion, bf16[512,512]{0,1:T(8,128)(2,1)S(1)} %all_gather.15, f32[512]{0:T(512)S(1)} %maximum_divide_fusion), kind=kOutput, calls=%fused_computation.7 | convolution fusion | flops 2150367232 | bytes 8914944 | tf_op jit(solution)/shard_map/dot_general | solution.py:11
  176.3 8.0 %all-to-all-start.5 = ((bf16[32,128,512]{2,1,0:T(8,128)(2,1)}), bf16[32,128,512]{2,1,0:T(8,128)(2,1)}, u32[]{:S(2)}, u32[]{:S(2)}) async-start(bf16[32,128,512]{2,1,0:T(8,128)(2,1)} %bitcast.97), calls=%async_computation.5 | async-start | bytes 8388608 | tf_op jit(solution)/shard_map/all_to_all | solution.py:15
  185.5 49.0 %all-to-all-done.5 = bf16[32,128,512]{2,1,0:T(8,128)(2,1)} async-done(((bf16[32,128,512]{2,1,0:T(8,128)(2,1)}), bf16[32,128,512]{2,1,0:T(8,128)(2,1)}, u32[]{:S(2)}, u32[]{:S(2)}) %all-to-all-start.5) | async-done | bytes 4194336 | tf_op jit(solution)/shard_map/all_to_all | solution.py:15
  235.4 3.5 %all-to-all-start.4 = ((bf16[512,4,128]{2,0,1:T(8,128)(2,1)}), bf16[512,4,128]{2,0,1:T(8,128)(2,1)S(1)}, u32[]{:S(2)}, u32[]{:S(2)}) async-start(bf16[512,4,128]{2,0,1:T(8,128)(2,1)} %tile.2), calls=%async_computation.4 | async-start | bytes 1048576 | tf_op jit(solution)/shard_map/all_to_all | solution.py:34
  241.7 6.3 %collective-permute-start = (f32[128,512]{1,0:T(8,128)S(1)}, f32[128,512]{1,0:T(8,128)S(1)}, u32[]{:S(2)}, u32[]{:S(2)}) collective-permute-start(f32[128,512]{1,0:T(8,128)S(1)} %convert_reduce_fusion), channel_id=1, source_target_pairs={{0,0},{1,4},{2,8},{3,12},{4,16},{5,20},{6,24},{7,28},{8,32},{9,36}... | collective-permute-start | bytes 786440 | tf_op jit(solution)/shard_map/ppermute | solution.py:98
  248.0 17.9 %all_gather.14 = bf16[512,512]{0,1:T(8,128)(2,1)S(1)} all-gather(bf16[512,128]{0,1:T(8,128)(2,1)S(1)} %get-tuple-element.58), channel_id=1, replica_groups=mesh['rel'=4,'ent'=32] {'rel'}, dimensions={1}, use_global_device_ids=true | all-gather | bytes 655360 | tf_op jit(solution)/shard_map/all_gather | solution.py:86
  (56 shorter events, 26.6 us)
Async XLA Ops:
  0.6 52.4 %copy-start = (bf16[512,512]{1,0:T(8,128)(2,1)S(1)}, bf16[512,512]{1,0:T(8,128)(2,1)}, u32[]{:S(2)}) copy-start(bf16[512,512]{1,0:T(8,128)(2,1)} %param.12) | copy-start | bytes 1572868
  45.5 11.8 %all-to-all-start = ((s32[32,1,128]{2,1,0:T(1,128)}), s32[32,1,128]{2,1,0:T(1,128)S(1)}, u32[]{:S(2)}, u32[]{:S(2)}) async-start(s32[32,1,128]{2,1,0:T(1,128)} %reshape.372), calls=%async_computation | async-start | bytes 32768 | tf_op jit(solution)/shard_map/all_to_all | solution.py:15
  57.3 15.9 %all-to-all-start.1 = ((bf16[32,64,128]{2,1,0:T(8,128)(2,1)}), bf16[32,64,128]{2,1,0:T(8,128)(2,1)S(1)}, u32[]{:S(2)}, u32[]{:S(2)}) async-start(bf16[32,64,128]{2,1,0:T(8,128)(2,1)} %bitcast.44), calls=%async_computation.1 | async-start | bytes 1048576 | tf_op jit(solution)/shard_map/all_to_all | solution.py:15
  64.0 6.2 %copy-start.4 = (f32[1000,32]{0,1:T(8,128)S(1)}, f32[1000,32]{0,1:T(8,128)}, u32[]{:S(2)}) copy-start(f32[1000,32]{0,1:T(8,128)} %param.15) | copy-start | bytes 384004
  80.4 14.0 %copy-start.2 = (bf16[32,128,512]{2,1,0:T(8,128)(2,1)S(1)}, bf16[32,128,512]{2,1,0:T(8,128)(2,1)}, u32[]{:S(2)}) copy-start(bf16[32,128,512]{2,1,0:T(8,128)(2,1)} %constant_dynamic-slice_fusion.1) | copy-start | bytes 12582916
  94.4 19.5 %copy-start.3 = (bf16[512,512]{1,0:T(8,128)(2,1)S(1)}, bf16[512,512]{1,0:T(8,128)(2,1)}, u32[]{:S(2)}) copy-start(bf16[512,512]{1,0:T(8,128)(2,1)} %param.13) | copy-start | bytes 1572868
  99.9 13.9 %all-to-all-start.2 = ((bf16[4,512,128]{1,2,0:T(8,128)(2,1)}), bf16[4,512,128]{1,2,0:T(8,128)(2,1)S(1)}, u32[]{:S(2)}, u32[]{:S(2)}) async-start(bf16[4,512,128]{1,2,0:T(8,128)(2,1)} %bitcast.51), calls=%async_computation.2 | async-start | bytes 1048576 | tf_op jit(solution)/shard_map/all_to_all | solution.py:15
  160.4 16.0 %all-to-all-start.3 = ((bf16[32,64,128]{2,1,0:T(8,128)(2,1)}), bf16[32,64,128]{2,1,0:T(8,128)(2,1)S(1)}, u32[]{:S(2)}, u32[]{:S(2)}) async-start(bf16[32,64,128]{2,1,0:T(8,128)(2,1)} %bitcast.54), calls=%async_computation.3 | async-start | bytes 1048576 | tf_op jit(solution)/shard_map/all_to_all | solution.py:15
  176.3 58.2 %all-to-all-start.5 = ((bf16[32,128,512]{2,1,0:T(8,128)(2,1)}), bf16[32,128,512]{2,1,0:T(8,128)(2,1)}, u32[]{:S(2)}, u32[]{:S(2)}) async-start(bf16[32,128,512]{2,1,0:T(8,128)(2,1)} %bitcast.97), calls=%async_computation.5 | async-start | bytes 8388608 | tf_op jit(solution)/shard_map/all_to_all | solution.py:15
  235.4 31.6 %all-to-all-start.4 = ((bf16[512,4,128]{2,0,1:T(8,128)(2,1)}), bf16[512,4,128]{2,0,1:T(8,128)(2,1)S(1)}, u32[]{:S(2)}, u32[]{:S(2)}) async-start(bf16[512,4,128]{2,0,1:T(8,128)(2,1)} %tile.2), calls=%async_computation.4 | async-start | bytes 1048576 | tf_op jit(solution)/shard_map/all_to_all | solution.py:34
  238.9 30.0 %copy-start.1 = (bf16[512,512]{1,0:T(8,128)(2,1)S(1)}, bf16[512,512]{1,0:T(8,128)(2,1)}, u32[]{:S(2)}) copy-start(bf16[512,512]{1,0:T(8,128)(2,1)} %param.12) | copy-start | bytes 1572868
  241.7 26.5 %collective-permute-start = (f32[128,512]{1,0:T(8,128)S(1)}, f32[128,512]{1,0:T(8,128)S(1)}, u32[]{:S(2)}, u32[]{:S(2)}) collective-permute-start(f32[128,512]{1,0:T(8,128)S(1)} %convert_reduce_fusion), channel_id=1, source_target_pairs={{0,0},{1,4},{2,8},{3,12},{4,16},{5,20},{6,24},{7,28},{8,32},{9,36}... | collective-permute-start | bytes 786440 | tf_op jit(solution)/shard_map/ppermute | solution.py:98
